TPU v7x, 32 devices: a whole 2x2x4 slice. The times are simulated.
32 devices in a mesh: vx: 4 (over y, x), vy: 8 (over z, core).
Axes of the slice: x: 2, y: 2, z: 4, core: 2. Of those that a mesh axis runs over, the one named last changes fastest.
Arguments:
- hidden: bfloat16 [128, 5120], P(('vx', 'vy')), may hold values from -96 to 96
- unembed: bfloat16 [152064, 5120], P(('vx', 'vy')), may hold values from -2 to 2
- loss_mask: int32 [128], P(('vx', 'vy')), may hold values 0 or 1
- seq_ids: int32 [128], P(('vx', 'vy')), may hold values from 0 to 7, never falling along the last dimension, each value on 1 to 32 neighbouring positions
Outputs:
- entropy: float32 [128], P(('vx', 'vy'))
- seq_mean: float32 [8], replicated
Inputs may be any that keep to these rules, and one draw needn't show every extreme that they name: `seq_ids`: sequence numbers never fall along the tokens; each sequence has 1 to 32 tokens.
All inputs are finite; a program needn't handle non-finite values. No bound on the sum of `loss_mask` on one device may be relied on, other than what follows from the above.
Results may differ from a plain program's by a relative error of at most 0.0013.
Values may be sent and summed in bfloat16 or wider, within the bound.
A program may use at most 128 MiB of HBM per device.

v0:
```python
import jax
import jax.numpy as jnp
from jax import lax
from jax.sharding import PartitionSpec as P

SEQS = 8


def sequence_sums(entropy_rows, mask_rows, id_rows):
    member = (id_rows[:, None] == jnp.arange(SEQS, dtype=jnp.int32)[None, :]) & (
        mask_rows[:, None] > 0
    )
    partial_sums = jnp.sum(entropy_rows[:, None] * member.astype(jnp.float32), axis=0)
    partial_counts = jnp.sum(member.astype(jnp.int32), axis=0)
    return (partial_sums, partial_counts)


def per_device(hidden, unembed, loss_mask, seq_ids):
    tok_local = hidden.shape[0]
    all_mask, all_ids = (
        lax.all_gather(loss_mask, ("vx", "vy"), axis=0, tiled=True),
        lax.all_gather(seq_ids, ("vx", "vy"), axis=0, tiled=True),
    )
    logits = lax.dot_general(
        unembed,
        lax.all_gather(hidden, ("vx", "vy"), axis=0, tiled=True),
        (((1,), (1,)), ((), ())),
        preferred_element_type=jnp.float32,
    )
    peaked = jnp.max(logits, axis=0)
    shifted = logits - peaked[None, :]
    expval = jnp.exp(shifted)
    stats = jnp.stack([peaked, jnp.sum(expval, axis=0), jnp.sum(expval * shifted, axis=0)])
    peaked, totals, tilted = (stats[0], stats[1], stats[2])
    position = lax.axis_index(("vx", "vy")) * tok_local
    largest = lax.pmax(peaked, ("vx", "vy"))
    shift = peaked - largest
    factor = jnp.exp(shift)
    norms_all, tilts_all = lax.psum(
        (factor * totals, factor * (tilted + shift * totals)), ("vx", "vy")
    )
    entropy_all = jnp.log(norms_all) - tilts_all / norms_all
    entropy = lax.dynamic_slice_in_dim(entropy_all, position, tok_local)
    seq_sums, seq_counts = sequence_sums(entropy_all, all_mask, all_ids)
    seq_mean = seq_sums / jnp.maximum(seq_counts, 1).astype(jnp.float32)
    return (entropy, seq_mean)


def solution(mesh):
    in_specs = (P(("vx", "vy"), None), P(("vx", "vy"), None), P(("vx", "vy")), P(("vx", "vy")))
    out_specs = (P(("vx", "vy")), P())
    return jax.shard_map(
        per_device, mesh=mesh, in_specs=in_specs, out_specs=out_specs, check_vma=False
    )
```

profile of v0, /device:TPU:0, one launch (start us, length us, event | category | flops | bytes accessed | tf_op | source)
XLA Modules:
  0.0 179.5 jit_solution(8160077383454973072)
XLA Ops:
  7.2 0.0 all-gather.3.cloned.1.call-start
  7.2 0.7 all-gather.3.cloned.1.call-update
  7.9 0.9 dynamic-update-slice
  8.8 0.8 dynamic-update-slice.1
  9.6 42.0 %all-reduce.2 = (s32[128]{0:T(128)S(1)}, s32[128]{0:T(128)S(1)}) all-reduce(s32[128]{0:T(128)S(1)} %dynamic-update-slice, s32[128]{0:T(128)S(1)} %dynamic-update-slice.1), channel_id=1, replica_groups=mesh['vx'=4,'vy'=8] {'vx','vy'}, use_global_device_ids=true, to_apply=%add | all-reduce | flops 256 | bytes 2048
  51.6 0.1 convert_reduce_fusion
  51.7 16.3 %all-gather.3.cloned.1.call-done = bf16[32,4,5120]{2,1,0:T(4,128)(2,1)} async-done(((bf16[1,4,5120]{2,1,0:T(4,128)(2,1)}), bf16[32,4,5120]{2,1,0:T(4,128)(2,1)}) %all-gather.3.cloned.1.call-update) | async-done | bytes 1310736 | tf_op jit(solution)/shard_map/all_gather | solution.py:26
  68.0 3.3 %reshape.14 = bf16[128,5120]{1,0:T(8,128)(2,1)} reshape(bf16[32,4,5120]{2,1,0:T(4,128)(2,1)} %all-gather.3.cloned.1.call-done) | data formatting | bytes 2621440
  71.3 20.4 %fusion.2 = (f32[128]{0:T(128)S(1)}, f32[4752,128]{1,0:T(8,128)S(1)}) fusion(bf16[4752,5120]{1,0:T(8,128)(2,1)} %param.5, bf16[128,5120]{1,0:T(8,128)(2,1)} %reshape.14), kind=kOutput, calls=%fused_computation.12 | convolution fusion | flops 6229149696 | bytes 52404736 | tf_op jit(solution)/shard_map/dot_general | solution.py:24
  91.7 39.1 %pmax.7 = f32[128]{0:T(128)S(1)} all-reduce(f32[128]{0:T(128)S(1)} %get-tuple-element.10), channel_id=1, replica_groups=mesh['vx'=4,'vy'=8] {'vx','vy'}, use_global_device_ids=true, to_apply=%region_1.0 | all-reduce | flops 128 | bytes 1024 | tf_op jit(solution)/shard_map/pmax | solution.py:36
  130.9 0.7 exponential_reduce_fusion
  131.5 39.9 %all-reduce.3 = (f32[128]{0:T(128)S(1)}, f32[128]{0:T(128)S(1)}) all-reduce(f32[128]{0:T(128)S(1)} %get-tuple-element.9, f32[128]{0:T(128)S(1)} %get-tuple-element.8), channel_id=1, replica_groups=mesh['vx'=4,'vy'=8] {'vx','vy'}, use_global_device_ids=true, to_apply=%region_5.0 | all-reduce | flops 256 | bytes 2048 | tf_op jit(solution)/shard_map/psum | solution.py:39
  171.5 0.1 select_reduce_fusion
  171.6 0.6 dynamic_slice.3
  172.2 0.5 convert_divide_fusion
  (5 shorter events, 0.0 us)
Async XLA Ops:
  7.2 60.9 %all-gather.3.cloned.1.call-start = ((), (), s32[]{:S(2)}) async-start(), calls=%async_computation | async-start | bytes 1351680 | tf_op jit(solution)/shard_map/all_gather | solution.py:26
Sparse Core Ops, SparseCore 0:
  10.8 57.1 all-gather.2
where the time goes:
time: 180 us
  blocking collectives  121 us (67%)
  matrix products  20.4 us (11%)
  waiting for transfers between devices  17 us (9%)
  between operations  14.1 us (8%)
  local copies, waits for them, and re-layouts  5.59 us (3%)
    unnamed x1, blocking collectives  42 us
    psum x1, blocking collectives, per_device(): lax.psum((factor * totals, factor * (tilted + shift * totals)), ('vx', 'v...  39.9 us
    pmax x1, blocking collectives, per_device(): largest = lax.pmax(peaked, ('vx', 'vy'))  39.1 us
    dot_general x1, matrix products, per_device(): lax.dot_general(unembed, lax.all_gather(hidden, ('vx', 'vy'), axis=0, til...  20.4 us
    all_gather x1, waiting for transfers between devices, per_device(): lax.all_gather(hidden, ('vx', 'vy'), axis=0, tiled=True)  16.3 us
    unnamed x5, local copies, waits for them, and re-layouts  5 us
  transfers between devices with their start and end apart: 1, of which 1 were waited for; matrix products, arithmetic and copies ran while one was open for 1% of the time, Pallas kernels for 0%

commit v1 on v0

--- a/solution.py
+++ b/solution.py
@@ -37,7 +37,7 @@
     shift = peaked - largest
     factor = jnp.exp(shift)
     norms_all, tilts_all = lax.psum(
-        (factor * totals, factor * (tilted + shift * totals)), ("vx", "vy")
+        lax.psum((factor * totals, factor * (tilted + shift * totals)), "vx"), "vy"
     )
     entropy_all = jnp.log(norms_all) - tilts_all / norms_all
     entropy = lax.dynamic_slice_in_dim(entropy_all, position, tok_local)

time: 180 us -> 164 us (0.911)
  blocking collectives: 121 us -> 105 us
    psum x1 -> x2, blocking collectives: 39.9 us -> 23.4 us  [the longest x1 13.6 us: per_device(): lax.psum(lax.psum((factor * totals, factor * (tilted + shift * totals)),...]
where the time goes in v1:
time: 164 us; the launch traced here: 163 us
  blocking collectives  105 us (64%)
  matrix products  20.4 us (12%)
  waiting for transfers between devices  17 us (10%)
  between operations  14.1 us (9%)
  local copies, waits for them, and re-layouts  5.59 us (3%)
    unnamed x1, blocking collectives  42 us
    pmax x1, blocking collectives, per_device(): largest = lax.pmax(peaked, ('vx', 'vy'))  39.2 us
    dot_general x1, matrix products, per_device(): lax.dot_general(unembed, lax.all_gather(hidden, ('vx', 'vy'), axis=0, til...  20.4 us
    all_gather x1, waiting for transfers between devices, per_device(): lax.all_gather(hidden, ('vx', 'vy'), axis=0, tiled=True)  16.3 us
    psum x1, blocking collectives, per_device(): lax.psum(lax.psum((factor * totals, factor * (tilted + shift * totals)),...  13.6 us
    psum x1, blocking collectives, per_device(): lax.psum((factor * totals, factor * (tilted + shift * totals)), 'vx')  9.8 us
    unnamed x5, local copies, waits for them, and re-layouts  5 us
  transfers between devices with their start and end apart: 1, of which 1 were waited for; matrix products, arithmetic and copies ran while one was open for 1% of the time, Pallas kernels for 0%

profile of v1, /device:TPU:0, one launch (start us, length us, event | category | flops | bytes accessed | tf_op | source)
XLA Modules:
  0.0 163.0 jit_solution(6698702954244121656)
XLA Ops:
  7.2 0.0 all-gather.3.cloned.1.call-start
  7.2 0.7 all-gather.3.cloned.1.call-update
  7.9 0.9 dynamic-update-slice
  8.8 0.8 dynamic-update-slice.1
  9.6 42.0 %all-reduce.2 = (s32[128]{0:T(128)S(1)}, s32[128]{0:T(128)S(1)}) all-reduce(s32[128]{0:T(128)S(1)} %dynamic-update-slice, s32[128]{0:T(128)S(1)} %dynamic-update-slice.1), channel_id=1, replica_groups=mesh['vx'=4,'vy'=8] {'vx','vy'}, use_global_device_ids=true, to_apply=%add | all-reduce | flops 256 | bytes 2048
  51.6 0.1 convert_reduce_fusion
  51.7 16.3 %all-gather.3.cloned.1.call-done = bf16[32,4,5120]{2,1,0:T(4,128)(2,1)} async-done(((bf16[1,4,5120]{2,1,0:T(4,128)(2,1)}), bf16[32,4,5120]{2,1,0:T(4,128)(2,1)}) %all-gather.3.cloned.1.call-update) | async-done | bytes 1310736 | tf_op jit(solution)/shard_map/all_gather | solution.py:26
  68.0 3.3 %reshape.14 = bf16[128,5120]{1,0:T(8,128)(2,1)} reshape(bf16[32,4,5120]{2,1,0:T(4,128)(2,1)} %all-gather.3.cloned.1.call-done) | data formatting | bytes 2621440
  71.3 20.4 %fusion.2 = (f32[128]{0:T(128)S(1)}, f32[4752,128]{1,0:T(8,128)S(1)}) fusion(bf16[4752,5120]{1,0:T(8,128)(2,1)} %param.5, bf16[128,5120]{1,0:T(8,128)(2,1)} %reshape.14), kind=kOutput, calls=%fused_computation.12 | convolution fusion | flops 6229149696 | bytes 52404736 | tf_op jit(solution)/shard_map/dot_general | solution.py:24
  91.7 39.2 %pmax.7 = f32[128]{0:T(128)S(1)} all-reduce(f32[128]{0:T(128)S(1)} %get-tuple-element.12), channel_id=1, replica_groups=mesh['vx'=4,'vy'=8] {'vx','vy'}, use_global_device_ids=true, to_apply=%region_1.0 | all-reduce | flops 128 | bytes 1024 | tf_op jit(solution)/shard_map/pmax | solution.py:36
  130.9 0.7 exponential_reduce_fusion
  131.6 9.8 %all-reduce.4 = (f32[128]{0:T(128)S(1)}, f32[128]{0:T(128)S(1)}) all-reduce(f32[128]{0:T(128)S(1)} %get-tuple-element.11, f32[128]{0:T(128)S(1)} %get-tuple-element.10), channel_id=1, replica_groups=mesh['vx'=4,'vy'=8] {'vx'}, use_global_device_ids=true, to_apply=%region_6.0 | all-reduce | flops 256 | bytes 2048 | tf_op jit(solution)/shard_map/psum | solution.py:40
  141.4 13.6 %all-reduce.3 = (f32[128]{0:T(128)S(1)}, f32[128]{0:T(128)S(1)}) all-reduce(f32[128]{0:T(128)S(1)} %get-tuple-element.8, f32[128]{0:T(128)S(1)} %get-tuple-element.9), channel_id=1, replica_groups=mesh['vx'=4,'vy'=8] {'vy'}, use_global_device_ids=true, to_apply=%region_7.0 | all-reduce | flops 256 | bytes 2048 | tf_op jit(solution)/shard_map/psum | solution.py:39
  154.9 0.1 select_reduce_fusion
  155.1 0.6 dynamic_slice.3
  155.6 0.5 convert_divide_fusion
  (5 shorter events, 0.0 us)
Async XLA Ops:
  7.2 60.9 %all-gather.3.cloned.1.call-start = ((), (), s32[]{:S(2)}) async-start(), calls=%async_computation | async-start | bytes 1351680 | tf_op jit(solution)/shard_map/all_gather | solution.py:26
Sparse Core Ops, SparseCore 0:
  10.8 57.1 all-gather.2
